TPU v7x, 32 devices: a whole 2x2x4 slice. The times are simulated.
32 devices in a mesh: zone: 4 (over y, x), slab: 8 (over z, core).
Axes of the slice: x: 2, y: 2, z: 4, core: 2. Of those that a mesh axis runs over, the one named last changes fastest.
Arguments:
- tracers: float32 [4, 4, 2048, 2048], P('zone', None, 'slab'), may hold values from -6 to 6
- velocity: float32 [4, 2, 2048, 2048], P('zone', None, 'slab'), may hold values from -0.2 to 0.2
- diffusivity: float32 [4], replicated, may hold values from 0.02 to 0.12
- owner_dev: int32 [512, 2], P('slab'), may hold values from 0 to 23, all different within a row; in each aligned block of 64 rows (0 to 63, 64 to 127, ...) at most 7 rows name the same one
- owner_seg: int32 [512, 2], P('slab'), may hold values from 0 to 63
- intersection: float32 [512, 2], P('slab'), may hold values from 0.2 to 1
Outputs:
- updated: float32 [4, 4, 2048, 2048], P('zone', None, 'slab')
Inputs may be any that keep to these rules, and one draw needn't show every extreme that they name: owner_dev names workpiece slab zone * 8 + slab; the 2 entries of a row differ; the rows of one pin slab name one workpiece slab at most 7 times, and some name one exactly 7 times.
All inputs are finite; a program needn't handle non-finite values.
Results may differ from a plain program's by a relative error of at most 0.00007.
Values sent between devices are 32-bit elements; how exact they have to be, the bound alone decides.
No kernel may reach another device: no remote copies, remote signals or barrier semaphores. Data moves between devices by JAX's collectives and lax.ppermute only.
A program may use at most 128 MiB of HBM per device.

v0:
```python
import jax
import jax.numpy as jnp
from jax import lax
from jax.sharding import PartitionSpec as P

SEG = 32
COUPLE = 0.5


def extended(block, sides, width):
    for axis, dim in sides:
        count = lax.axis_size(axis)
        forward = [(i, i + 1) for i in range(count - 1)]
        backward = [(target, source) for source, target in forward]
        low = lax.ppermute(
            lax.slice_in_dim(block, block.shape[dim] - width, None, axis=dim), axis, forward
        )
        high = lax.ppermute(lax.slice_in_dim(block, 0, width, axis=dim), axis, backward)
        block = jnp.concatenate([low, block, high], axis=dim)
    return block


def from_root(block, axis, owner):
    block = jnp.where(lax.axis_index(axis) == owner, block, jnp.zeros_like(block))
    return lax.psum(block, axis)


def advance(center, upper_row, lower_row, velocity, diffusivity):
    left_cells = jnp.roll(center, 1, axis=3)
    right_cells = jnp.roll(center, -1, axis=3)
    along_rows = velocity[:, 0][:, None]
    along_cols = velocity[:, 1][:, None]
    transport = jnp.maximum(along_rows, 0.0) * (center - upper_row) + jnp.minimum(
        along_rows, 0.0
    ) * (lower_row - center)
    transport = (
        transport
        + jnp.maximum(along_cols, 0.0) * (center - left_cells)
        + jnp.minimum(along_cols, 0.0) * (right_cells - center)
    )
    laplace = upper_row + lower_row + left_cells + right_cells - 4.0 * center
    return center + diffusivity[None, :, None, None] * laplace - transport


def shards(tracers, velocity, diffusivity, owner_dev, owner_seg, intersection):
    zone_count = lax.axis_size("zone")
    slab_count = lax.axis_size("slab")
    zone_index = lax.axis_index("zone")
    padded = extended(tracers, (("slab", 2),), 1)
    stepped = advance(
        padded[:, :, 1:-1], padded[:, :, :-2], padded[:, :, 2:], velocity, diffusivity
    )
    tracer_count = tracers.shape[1]
    row_count = tracers.shape[2]
    col_count = tracers.shape[3]
    seg_count = col_count // SEG
    payload = tracer_count * SEG
    own_face = (
        tracers[0, :, row_count - 1, :]
        .reshape(tracer_count, seg_count, SEG)
        .transpose(1, 0, 2)
        .reshape(seg_count, payload)
    )
    pin_face = from_root(own_face, "zone", zone_count - 1)
    fanout = owner_dev.shape[1]
    item_count = owner_dev.shape[0] * fanout
    target_dev = owner_dev.reshape(item_count)
    target_seg = owner_seg.reshape(item_count)
    weight = intersection.reshape(item_count)
    in_zone = target_dev // slab_count == zone_index
    target_slab = target_dev % slab_count
    pin_values = jnp.repeat(pin_face, fanout, axis=0)
    highest = lax.Precision.HIGHEST
    zone_faces = lax.all_gather(own_face, "slab", axis=0, tiled=True)
    slot_ids = jnp.arange(slab_count * seg_count, dtype=jnp.int32)
    picker = (
        ((target_slab * seg_count + target_seg)[:, None] == slot_ids[None, :]) & in_zone[:, None]
    ).astype(jnp.float32)
    owner_values = jnp.dot(picker, zone_faces, precision=highest)
    item_flux = jnp.where(in_zone, weight, 0.0)[:, None] * (pin_values - owner_values)
    inflow = lax.psum_scatter(
        jnp.dot(picker.T, item_flux, precision=highest), "slab", scatter_dimension=0, tiled=True
    )
    pin_part = jnp.sum(item_flux.reshape(seg_count, fanout, payload), axis=1)
    pin_total = lax.psum(pin_part, "zone")
    is_pin = zone_index == zone_count - 1
    coupling = COUPLE * inflow - jnp.where(is_pin, COUPLE * pin_total, 0.0)
    coupling = (
        coupling.reshape(seg_count, tracer_count, SEG)
        .transpose(1, 0, 2)
        .reshape(tracer_count, col_count)
    )
    return stepped.at[0, :, row_count - 1, :].add(coupling)


def solution(mesh):
    placed = (
        P("zone", None, "slab", None),
        P("zone", None, "slab", None),
        P(),
        P("slab", None),
        P("slab", None),
        P("slab", None),
    )
    return jax.shard_map(
        shards, mesh=mesh, in_specs=placed, out_specs=P("zone", None, "slab", None), check_vma=False
    )
```

profile of v0, /device:TPU:8, one launch (start us, length us, event | category | flops | bytes accessed | tf_op | source)
XLA Modules:
  0.0 117.2 jit_solution(10784930607515676139)
XLA Ops:
  6.5 0.0 reduce-scatter.2.cloned.1.call-start
  6.5 1.2 slice_reduce_fusion
  7.7 0.1 reshape_squeeze.3
  7.8 0.1 copy.60
  7.9 0.1 copy.61
  7.9 14.4 %all_gather.3 = f32[512,128]{1,0:T(8,128)S(1)} all-gather(f32[64,128]{1,0:T(8,128)S(1)} %copy.61), channel_id=1, replica_groups=mesh['zone'=4,'slab'=8] {'slab'}, dimensions={0}, use_global_device_ids=true | all-gather | bytes 294912 | tf_op jit(solution)/shard_map/all_gather | solution.py:74
  22.4 16.3 %psum.14 = f32[64,128]{1,0:T(8,128)S(1)} all-reduce(f32[64,128]{1,0:T(8,128)S(1)} %broadcast_select_fusion.1), channel_id=1, replica_groups=mesh['zone'=4,'slab'=8] {'zone'}, use_global_device_ids=true, to_apply=%region_1.2 | all-reduce | flops 8192 | bytes 65536 | tf_op jit(solution)/shard_map/psum | solution.py:25
  38.7 0.8 copy.57
  39.5 0.1 reshape.148
  39.6 0.8 copy.59
  40.4 0.1 reshape.150
  40.5 0.8 copy.58
  41.3 0.1 reshape.149
  41.5 0.3 fusion.14
  41.8 1.2 fusion.16
  43.0 0.0 reduce-scatter.2.cloned.1.call-update
  43.0 1.9 %collective-permute-start = (f32[1,4,1,2048]{3,2,1,0:T(1,128)S(1)}, f32[1,4,1,2048]{3,2,1,0:T(1,128)S(1)}, u32[]{:S(2)}, u32[]{:S(2)}) collective-permute-start(f32[1,4,1,2048]{3,2,1,0:T(1,128)S(1)} %get-tuple-element.21), channel_id=1, source_target_pairs={{0,1},{1,2},{2,3},{3,4},{4,5},{5,6},{6,7},{8,9},{9,10},{10,11},{11... | collective-permute-start | bytes 98312 | tf_op jit(solution)/shard_map/ppermute | solution.py:15
  44.9 0.0 copy-start
  44.9 3.9 %collective-permute-start.1 = (f32[1,4,1,2048]{3,2,1,0:T(1,128)S(1)}, f32[1,4,1,2048]{3,2,1,0:T(1,128)S(1)}, u32[]{:S(2)}, u32[]{:S(2)}) collective-permute-start(f32[1,4,1,2048]{3,2,1,0:T(1,128)S(1)} %get-tuple-element.20), channel_id=1, source_target_pairs={{1,0},{2,1},{3,2},{4,3},{5,4},{6,5},{7,6},{9,8},{10,9},{11,10},{12... | collective-permute-start | bytes 98312 | tf_op jit(solution)/shard_map/ppermute | solution.py:18
  48.9 13.3 %fusion.28 = (f32[1,4,256,2047]{3,2,1,0:T(8,128)}, f32[1,4,256,2047]{3,2,1,0:T(8,128)}) fusion(f32[1,4,256,2048]{3,2,1,0:T(8,128)} %param.8), kind=kLoop, calls=%fused_computation.47 | loop fusion | bytes 33538048 | tf_op jit(solution)/shard_map/jit(_roll_static)/slice | solution.py:29
  62.1 0.0 copy-start.2
  62.1 0.0 copy-start.1
  62.1 1.4 %fusion.27 = (f32[1,4,256,1]{3,2,1,0:T(8,128)S(1)}, f32[1,4,256,1]{3,2,1,0:T(8,128)S(1)}) fusion(f32[1,4,256,2048]{3,2,1,0:T(8,128)} %param.8), kind=kLoop, calls=%fused_computation.46 | loop fusion | bytes 16384 | tf_op jit(solution)/shard_map/jit(_roll_static)/slice | solution.py:29
  63.6 0.0 copy-done
  63.6 2.9 %maximum_bitcast_fusion.1 = (f32[256,2048]{1,0:T(8,128)S(1)}, f32[256,2048]{1,0:T(8,128)}, f32[256,2048]{1,0:T(8,128)}, f32[256,2048]{1,0:T(8,128)}) fusion(f32[1,2,256,2048]{3,2,1,0:T(8,128)S(1)} %copy-done), kind=kLoop, calls=%fused_computation.21 | loop fusion | flops 2097152 | bytes 12582912 | tf_op jit(solution)/shard_map/mul | solution.py:33
  66.5 0.6 fusion.29
  67.1 0.0 copy-done.2
  67.1 2.0 %and_reduce_fusion = pred[]{:T(512)} fusion(s32[4]{0:T(128)S(1)} %copy-done.2, s32[1]{0:T(128)} %constant.60.clone.1, s32[1]{0:T(128)} %get-tuple-element.31, s32[1]{0:T(128)} %get-tuple-element.30), kind=kLoop, calls=%fused_computation.36 | loop fusion | flops 27 | bytes 29 | tf_op jit(solution)/shard_map/reduce.1
  69.1 0.1 reduce_sum.9
  69.2 14.3 %psum.15 = f32[64,128]{1,0:T(8,128)S(1)} all-reduce(f32[64,128]{1,0:T(8,128)S(1)} %reduce_sum.9), channel_id=1, replica_groups=mesh['zone'=4,'slab'=8] {'zone'}, use_global_device_ids=true, to_apply=%region_4.5 | all-reduce | flops 8192 | bytes 65536 | tf_op jit(solution)/shard_map/psum | solution.py:85
  83.5 0.0 collective-permute-done
  83.5 0.0 collective-permute-done.1
  83.5 0.0 copy-done.1
  83.5 21.2 %fusion.6 = f32[1,4,256,2048]{3,2,1,0:T(8,128)} fusion(f32[1,4,256,2048]{3,2,1,0:T(8,128)} %param.8, f32[1,4,1,2048]{3,2,1,0:T(1,128)S(1)} %collective-permute-done.1, f32[1,4,1,2048]{3,2,1,0:T(1,128)S(1)} %collective-permute-done, f32[1,4,256,1]{3,2,1,0:T(8,128)S(1)} %get-tuple-element.23, f32[1,4,256,2047]{3,2,1,0:T(8,128)} %get-tuple-element.25, ...), kind=kLoop, calls=%fused_computation.7 | loop fusion | flops 48234496 | bytes 42008592 | tf_op jit(solution)/shard_map/sub | solution.py:42
  104.7 0.0 reduce-scatter.2.cloned.1.call-done
  104.7 0.8 select_subtract_fusion
  105.5 0.1 copy.63
  105.6 0.1 copy.64
  105.7 0.1 reshape.156
  105.8 2.2 %broadcast_select_fusion = f32[1,4,1,2048]{3,2,1,0:T(1,128)S(1)} fusion(pred[]{:T(512)} %and_reduce_fusion, f32[1,4,1,2048]{3,2,1,0:T(1,128)S(1)} %reshape.156, f32[1,4,256,2048]{3,2,1,0:T(8,128)} %fusion.6, s32[]{:T(128)} %bitcast.4), kind=kLoop, calls=%fused_computation.31 | loop fusion | flops 16384 | bytes 98309 | tf_op jit(solution)/shard_map/select.1
  108.0 2.4 %scatter-add.4 = f32[1,4,256,2048]{3,2,1,0:T(8,128)} dynamic-update-slice(f32[1,4,256,2048]{3,2,1,0:T(8,128)} %fusion.6, f32[1,4,1,2048]{3,2,1,0:T(1,128)S(1)} %broadcast_select_fusion, s32[]{:T(128)} %constant.58.clone.1, s32[]{:T(128)} %constant.58.clone.1, s32[]{:T(128)} %bitcast.4, s32[]{:T(128)} %constant.58.clone.1) | dynamic-update-slice | bytes 65540 | tf_op jit(solution)/shard_map/scatter-add | solution.py:93
  (5 shorter events, 0.1 us)
Async XLA Ops:
  6.5 98.2 %reduce-scatter.2.cloned.1.call-start = ((), (), s32[]{:S(2)}) async-start(), calls=%async_computation.1 | async-start | bytes 294912 | tf_op jit(solution)/shard_map/reduce_scatter | solution.py:81
  43.0 40.5 %collective-permute-start = (f32[1,4,1,2048]{3,2,1,0:T(1,128)S(1)}, f32[1,4,1,2048]{3,2,1,0:T(1,128)S(1)}, u32[]{:S(2)}, u32[]{:S(2)}) collective-permute-start(f32[1,4,1,2048]{3,2,1,0:T(1,128)S(1)} %get-tuple-element.21), channel_id=1, source_target_pairs={{0,1},{1,2},{2,3},{3,4},{4,5},{5,6},{6,7},{8,9},{9,10},{10,11},{11... | collective-permute-start | bytes 98312 | tf_op jit(solution)/shard_map/ppermute | solution.py:15
  44.9 18.7 %copy-start = (f32[1,2,256,2048]{3,2,1,0:T(8,128)S(1)}, f32[1,2,256,2048]{3,2,1,0:T(8,128)}, u32[]{:S(2)}) copy-start(f32[1,2,256,2048]{3,2,1,0:T(8,128)} %param.9) | copy-start | bytes 12582916
  44.9 38.5 %collective-permute-start.1 = (f32[1,4,1,2048]{3,2,1,0:T(1,128)S(1)}, f32[1,4,1,2048]{3,2,1,0:T(1,128)S(1)}, u32[]{:S(2)}, u32[]{:S(2)}) collective-permute-start(f32[1,4,1,2048]{3,2,1,0:T(1,128)S(1)} %get-tuple-element.20), channel_id=1, source_target_pairs={{1,0},{2,1},{3,2},{4,3},{5,4},{6,5},{7,6},{9,8},{10,9},{11,10},{12... | collective-permute-start | bytes 98312 | tf_op jit(solution)/shard_map/ppermute | solution.py:18
  62.1 5.0 %copy-start.2 = (s32[4]{0:T(128)S(1)}, s32[4]{0:T(128)}, u32[]{:S(2)}) copy-start(s32[4]{0:T(128)} %constant.61.clone.1) | copy-start | bytes 52
  62.1 21.4 %copy-start.1 = (f32[4]{0:T(128)S(1)}, f32[4]{0:T(128)}, u32[]{:S(2)}) copy-start(f32[4]{0:T(128)} %param.10) | copy-start | bytes 52
Sparse Core Ops, SparseCore 0:
  43.1 26.0 reduce-scatter.1
where the time goes:
time: 118 us; the launch traced here: 117 us
  blocking collectives  45 us (38%)
  other arithmetic  29.1 us (25%)
  local copies, waits for them, and re-layouts  22.2 us (19%)
  between operations  13.5 us (11%)
  starting transfers between devices  5.83 us (5%)
  matrix products  1.48 us (1%)
    sub x1, other arithmetic, advance(): return center + diffusivity[None, :, None, None] * laplace - transport  21.2 us
    psum x1, blocking collectives, from_root(): return lax.psum(block, axis)  16.3 us
    slice x2, local copies, waits for them, and re-layouts, advance(): left_cells = jnp.roll(center, 1, axis=3)  14.7 us
    all_gather x1, blocking collectives, shards(): zone_faces = lax.all_gather(own_face, 'slab', axis=0, tiled=True)  14.4 us
    psum x1, blocking collectives, shards(): pin_total = lax.psum(pin_part, 'zone')  14.3 us
    another operation x3, other arithmetic  4.18 us
    ppermute x1, starting transfers between devices, extended(): lax.ppermute(lax.slice_in_dim(block, 0, width, axis=dim), axis, backward)  3.91 us
    mul x1, other arithmetic, advance(): jnp.maximum(along_rows, 0.0) * (center - upper_row)  2.91 us
  transfers between devices with their start and end apart: 3, of which 0 were waited for; matrix products, arithmetic and copies ran while one was open for 35% of the time, Pallas kernels for 0%

commit v1 on v0

--- a/solution.py
+++ b/solution.py
@@ -71,7 +71,16 @@
     target_slab = target_dev % slab_count
     pin_values = jnp.repeat(pin_face, fanout, axis=0)
     highest = lax.Precision.HIGHEST
-    zone_faces = lax.all_gather(own_face, "slab", axis=0, tiled=True)
+    ways = lax.axis_size("slab")
+    up = [(d, (d + 1) % ways) for d in range(ways)]
+    down = [(d, (d - 1) % ways) for d in range(ways)]
+    earlier, later = ([own_face], [own_face])
+    for _ in range(ways // 2):
+        earlier.append(lax.ppermute(earlier[-1], "slab", up))
+    for _ in range((ways - 1) // 2):
+        later.append(lax.ppermute(later[-1], "slab", down))
+    line = jnp.concatenate([*earlier[::-1], *later[1:]], axis=0)
+    zone_faces = jnp.roll(line, (lax.axis_index("slab") - ways // 2) * own_face.shape[0], axis=0)
     slot_ids = jnp.arange(slab_count * seg_count, dtype=jnp.int32)
     picker = (
         ((target_slab * seg_count + target_seg)[:, None] == slot_ids[None, :]) & in_zone[:, None]

time: 118 us -> 124 us (1.051)
  the two profiles are of different devices: /device:TPU:8 before, /device:TPU:0 now
where the time goes in v1:
time: 124 us; the launch traced here: 123 us
  other arithmetic  32.9 us (27%)
  blocking collectives  32.1 us (26%)
  local copies, waits for them, and re-layouts  23.5 us (19%)
  starting transfers between devices  15.1 us (12%)
  between operations  13.6 us (11%)
  waiting for transfers between devices  3.33 us (3%)
  matrix products  2.54 us (2%)
    sub x1, other arithmetic, advance(): return center + diffusivity[None, :, None, None] * laplace - transport  21.4 us
    psum x1, blocking collectives, from_root(): return lax.psum(block, axis)  17.9 us
    slice x2, local copies, waits for them, and re-layouts, advance(): left_cells = jnp.roll(center, 1, axis=3)  14.7 us
    psum x1, blocking collectives, shards(): pin_total = lax.psum(pin_part, 'zone')  14.2 us
    ppermute x3, starting transfers between devices, shards(): later.append(lax.ppermute(later[-1], 'slab', down))  10.2 us
    mul x1, other arithmetic, advance(): jnp.maximum(along_rows, 0.0) * (center - upper_row)  5.35 us
    another operation x3, other arithmetic  4.73 us
    ppermute x4, waiting for transfers between devices, shards(): earlier.append(lax.ppermute(earlier[-1], 'slab', up))  3.28 us
  transfers between devices with their start and end apart: 10, of which 2 were waited for; matrix products, arithmetic and copies ran while one was open for 42% of the time, Pallas kernels for 0%

profile of v1, /device:TPU:0, one launch (start us, length us, event | category | flops | bytes accessed | tf_op | source)
XLA Modules:
  0.0 123.0 jit_solution(18359484680694840704)
XLA Ops:
  6.5 1.7 %slice_reduce_fusion = (f32[4,2048]{1,0:T(4,128)S(1)}, f32[1,4,1,2048]{3,2,1,0:T(1,128)}, f32[1,4,1,2048]{3,2,1,0:T(1,128)}) fusion(f32[1,4,256,2048]{3,2,1,0:T(8,128)} %param.8), kind=kLoop, calls=%fused_computation.47 | loop fusion | bytes 163840 | tf_op jit(solution)/shard_map/slice | solution.py:16
  8.3 0.1 reshape_squeeze.3
  8.4 0.1 copy.37
  8.5 0.5 collective-permute-start.2
  9.0 4.1 %collective-permute-start.6 = (f32[64,128]{0,1:T(8,128)S(1)}, f32[64,128]{0,1:T(8,128)S(1)}, u32[]{:S(2)}, u32[]{:S(2)}) collective-permute-start(f32[64,128]{0,1:T(8,128)S(1)} %bitcast.18), channel_id=1, source_target_pairs={{0,7},{1,0},{2,1},{3,2},{4,3},{5,4},{6,5},{7,6},{8,15},{9,8},{10,9... | collective-permute-start | bytes 98312 | tf_op jit(solution)/shard_map/ppermute | solution.py:81
  13.1 1.9 %collective-permute-start = (f32[1,4,1,2048]{3,2,1,0:T(1,128)}, f32[1,4,1,2048]{3,2,1,0:T(1,128)}, u32[]{:S(2)}, u32[]{:S(2)}) collective-permute-start(f32[1,4,1,2048]{3,2,1,0:T(1,128)} %get-tuple-element.21), channel_id=1, source_target_pairs={{0,1},{1,2},{2,3},{3,4},{4,5},{5,6},{6,7},{8,9},{9,10},{10,11},{11... | collective-permute-start | bytes 98312 | tf_op jit(solution)/shard_map/ppermute | solution.py:15
  15.0 1.3 %collective-permute-start.1 = (f32[1,4,1,2048]{3,2,1,0:T(1,128)}, f32[1,4,1,2048]{3,2,1,0:T(1,128)}, u32[]{:S(2)}, u32[]{:S(2)}) collective-permute-start(f32[1,4,1,2048]{3,2,1,0:T(1,128)} %get-tuple-element.20), channel_id=1, source_target_pairs={{1,0},{2,1},{3,2},{4,3},{5,4},{6,5},{7,6},{9,8},{10,9},{11,10},{12... | collective-permute-start | bytes 98312 | tf_op jit(solution)/shard_map/ppermute | solution.py:18
  16.3 0.1 copy.38
  16.3 0.0 copy-start
  16.3 0.0 copy-start.1
  16.3 0.0 copy-start.2
  16.4 13.3 %fusion.30 = (f32[1,4,256,2047]{3,2,1,0:T(8,128)}, f32[1,4,256,2047]{3,2,1,0:T(8,128)}) fusion(f32[1,4,256,2048]{3,2,1,0:T(8,128)} %param.8), kind=kLoop, calls=%fused_computation.49 | loop fusion | bytes 33538048 | tf_op jit(solution)/shard_map/jit(_roll_static)/slice | solution.py:29
  29.6 1.4 %fusion.29 = (f32[1,4,256,1]{3,2,1,0:T(8,128)S(1)}, f32[1,4,256,1]{3,2,1,0:T(8,128)S(1)}) fusion(f32[1,4,256,2048]{3,2,1,0:T(8,128)} %param.8), kind=kLoop, calls=%fused_computation.48 | loop fusion | bytes 16384 | tf_op jit(solution)/shard_map/jit(_roll_static)/slice | solution.py:29
  31.1 0.1 copy.34
  31.2 0.1 reshape.148
  31.3 0.1 copy.36
  31.4 0.1 reshape.150
  31.5 0.1 copy.35
  31.6 0.1 reshape.149
  31.8 5.3 %maximum_bitcast_fusion.1 = (f32[256,2048]{1,0:T(8,128)S(1)}, f32[256,2048]{1,0:T(8,128)}, f32[256,2048]{1,0:T(8,128)}, f32[256,2048]{1,0:T(8,128)}) fusion(f32[1,2,256,2048]{3,2,1,0:T(8,128)} %param.9), kind=kLoop, calls=%fused_computation.21 | loop fusion | flops 2097152 | bytes 12582912 | tf_op jit(solution)/shard_map/mul | solution.py:33
  37.1 0.6 broadcast_select_fusion.1
  37.8 0.0 collective-permute-done.2
  37.8 1.2 collective-permute-start.3
  39.0 0.0 collective-permute-done.6
  39.0 2.5 %collective-permute-start.7 = (f32[64,128]{0,1:T(8,128)S(1)}, f32[64,128]{0,1:T(8,128)S(1)}, u32[]{:S(2)}, u32[]{:S(2)}) collective-permute-start(f32[64,128]{0,1:T(8,128)S(1)} %collective-permute-done.6), channel_id=1, source_target_pairs={{0,7},{1,0},{2,1},{3,2},{4,3},{5,4},{6,5},{7,6},{8,15},{9,8},{10,9... | collective-permute-start | bytes 98312 | tf_op jit(solution)/shard_map/ppermute | solution.py:81
  41.5 1.9 %collective-permute-done.3 = f32[64,128]{0,1:T(8,128)S(1)} collective-permute-done((f32[64,128]{0,1:T(8,128)S(1)}, f32[64,128]{0,1:T(8,128)S(1)}, u32[]{:S(2)}, u32[]{:S(2)}) %collective-permute-start.3) | collective-permute-done | bytes 32800 | tf_op jit(solution)/shard_map/ppermute | solution.py:79
  43.4 0.0 collective-permute-start.4
  43.4 0.6 fusion.31
  44.0 3.5 %collective-permute-start.8 = (f32[64,128]{0,1:T(8,128)S(1)}, f32[64,128]{0,1:T(8,128)}, u32[]{:S(2)}, u32[]{:S(2)}) collective-permute-start(f32[64,128]{0,1:T(8,128)S(1)} %collective-permute-done.7), channel_id=1, source_target_pairs={{0,7},{1,0},{2,1},{3,2},{4,3},{5,4},{6,5},{7,6},{8,15},{9,8},{10,9... | collective-permute-start | bytes 98312 | tf_op jit(solution)/shard_map/ppermute | solution.py:81
  47.6 1.4 %collective-permute-done.4 = f32[64,128]{0,1:T(8,128)S(1)} collective-permute-done((f32[64,128]{0,1:T(8,128)S(1)}, f32[64,128]{0,1:T(8,128)S(1)}, u32[]{:S(2)}, u32[]{:S(2)}) %collective-permute-start.4) | collective-permute-done | bytes 32800 | tf_op jit(solution)/shard_map/ppermute | solution.py:79
  49.0 0.0 collective-permute-start.5
  49.0 2.6 %and_reduce_fusion = pred[]{:T(512)} fusion(s32[4]{0:T(128)} %constant.84.clone.1, s32[1]{0:T(128)} %constant.83.clone.1, s32[1]{0:T(128)} %get-tuple-element.31, s32[1]{0:T(128)} %get-tuple-element.30), kind=kLoop, calls=%fused_computation.37 | loop fusion | flops 27 | bytes 29 | tf_op jit(solution)/shard_map/reduce.1
  51.5 17.9 %psum.14 = f32[64,128]{1,0:T(8,128)} all-reduce(f32[64,128]{1,0:T(8,128)} %broadcast_select_fusion.1), channel_id=1, replica_groups=mesh['zone'=4,'slab'=8] {'zone'}, use_global_device_ids=true, to_apply=%region_1.2 | all-reduce | flops 8192 | bytes 65536 | tf_op jit(solution)/shard_map/psum | solution.py:25
  69.5 2.0 %concatenate.30 = f32[1024,128]{0,1:T(8,128)} concatenate(f32[64,128]{0,1:T(8,128)} %collective-permute-done.5, f32[64,128]{0,1:T(8,128)S(1)} %collective-permute-done.4, f32[64,128]{0,1:T(8,128)S(1)} %collective-permute-done.3, f32[64,128]{0,1:T(8,128)S(1)} %collective-permute-done.2, f32[64,128]{0,1:T(8,128)S(1)} %bitcast.20, f32[64,128]{0,1:T(8,128)S(1)} %collective-permute-done.6, ...), dimensions={0} | concatenate | bytes 1048576 | tf_op jit(solution)/shard_map/jit(_roll_dynamic)/concatenate | solution.py:83
  71.5 0.8 broadcast_in_dim.19
  72.2 1.4 %fusion.14 = f32[128,128]{1,0:T(8,128)S(1)} fusion(f32[128,128]{1,0:T(8,128)S(1)} %bitcast.25, f32[1024,128]{0,1:T(8,128)} %concatenate.30, s32[]{:T(128)S(6)} %select_n.63, s32[128]{0:T(128)S(1)} %fusion.25, pred[128]{0:T(512)(128)(4,1)S(1)} %get-tuple-element.18, f32[128]{0:T(128)S(1)} %get-tuple-element.17), kind=kOutput, calls=%fused_computation.23 | convolution fusion | flops 100827136 | bytes 394372 | tf_op jit(solution)/shard_map/dot_general | solution.py:88
  73.6 1.2 fusion.17
  74.8 0.0 reduce-scatter.2.cloned.1.call-update
  74.8 21.4 %fusion.6 = f32[1,4,256,2048]{3,2,1,0:T(8,128)} fusion(f32[1,4,256,2048]{3,2,1,0:T(8,128)} %param.8, f32[1,4,1,2048]{3,2,1,0:T(1,128)} %collective-permute-done.1, f32[1,4,1,2048]{3,2,1,0:T(1,128)} %collective-permute-done, f32[1,4,256,1]{3,2,1,0:T(8,128)S(1)} %get-tuple-element.23, f32[1,4,256,2047]{3,2,1,0:T(8,128)} %get-tuple-element.25, ...), kind=kLoop, calls=%fused_computation.7 | loop fusion | flops 48234496 | bytes 42008592 | tf_op jit(solution)/shard_map/sub | solution.py:42
  96.2 0.1 reduce_sum.9
  96.3 14.2 %psum.15 = f32[64,128]{1,0:T(8,128)S(1)} all-reduce(f32[64,128]{1,0:T(8,128)S(1)} %reduce_sum.9), channel_id=1, replica_groups=mesh['zone'=4,'slab'=8] {'zone'}, use_global_device_ids=true, to_apply=%region_4.5 | all-reduce | flops 8192 | bytes 65536 | tf_op jit(solution)/shard_map/psum | solution.py:94
  110.5 0.0 reduce-scatter.2.cloned.1.call-done
  110.5 0.8 select_subtract_fusion
  111.3 0.1 copy.39
  111.4 0.1 copy.40
  111.5 0.1 reshape.156
  111.6 2.2 %broadcast_select_fusion = f32[1,4,1,2048]{3,2,1,0:T(1,128)S(1)} fusion(pred[]{:T(512)} %and_reduce_fusion, f32[1,4,1,2048]{3,2,1,0:T(1,128)S(1)} %reshape.156, f32[1,4,256,2048]{3,2,1,0:T(8,128)} %fusion.6, s32[]{:T(128)} %bitcast.4), kind=kLoop, calls=%fused_computation.32 | loop fusion | flops 16384 | bytes 98309 | tf_op jit(solution)/shard_map/select.1
  113.8 2.4 %scatter-add.4 = f32[1,4,256,2048]{3,2,1,0:T(8,128)} dynamic-update-slice(f32[1,4,256,2048]{3,2,1,0:T(8,128)} %fusion.6, f32[1,4,1,2048]{3,2,1,0:T(1,128)S(1)} %broadcast_select_fusion, s32[]{:T(128)} %constant.81.clone.1, s32[]{:T(128)} %constant.81.clone.1, s32[]{:T(128)} %bitcast.4, s32[]{:T(128)} %constant.81.clone.1) | dynamic-update-slice | bytes 65540 | tf_op jit(solution)/shard_map/scatter-add | solution.py:102
  (14 shorter events, 0.1 us)
Async XLA Ops:
  6.5 104.0 %reduce-scatter.2.cloned.1.call-start = ((), (), s32[]{:S(2)}) async-start(), calls=%async_computation.1 | async-start | bytes 294912 | tf_op jit(solution)/shard_map/reduce_scatter | solution.py:90
  8.5 29.3 %collective-permute-start.2 = (f32[64,128]{0,1:T(8,128)S(1)}, f32[64,128]{0,1:T(8,128)S(1)}, u32[]{:S(2)}, u32[]{:S(2)}) collective-permute-start(f32[64,128]{0,1:T(8,128)S(1)} %bitcast.17), channel_id=1, source_target_pairs={{0,1},{1,2},{2,3},{3,4},{4,5},{5,6},{6,7},{7,0},{8,9},{9,10},{10,1... | collective-permute-start | bytes 98312 | tf_op jit(solution)/shard_map/ppermute | solution.py:79
  9.0 30.0 %collective-permute-start.6 = (f32[64,128]{0,1:T(8,128)S(1)}, f32[64,128]{0,1:T(8,128)S(1)}, u32[]{:S(2)}, u32[]{:S(2)}) collective-permute-start(f32[64,128]{0,1:T(8,128)S(1)} %bitcast.18), channel_id=1, source_target_pairs={{0,7},{1,0},{2,1},{3,2},{4,3},{5,4},{6,5},{7,6},{8,15},{9,8},{10,9... | collective-permute-start | bytes 98312 | tf_op jit(solution)/shard_map/ppermute | solution.py:81
  13.1 61.7 %collective-permute-start = (f32[1,4,1,2048]{3,2,1,0:T(1,128)}, f32[1,4,1,2048]{3,2,1,0:T(1,128)}, u32[]{:S(2)}, u32[]{:S(2)}) collective-permute-start(f32[1,4,1,2048]{3,2,1,0:T(1,128)} %get-tuple-element.21), channel_id=1, source_target_pairs={{0,1},{1,2},{2,3},{3,4},{4,5},{5,6},{6,7},{8,9},{9,10},{10,11},{11... | collective-permute-start | bytes 98312 | tf_op jit(solution)/shard_map/ppermute | solution.py:15
  15.0 59.9 %collective-permute-start.1 = (f32[1,4,1,2048]{3,2,1,0:T(1,128)}, f32[1,4,1,2048]{3,2,1,0:T(1,128)}, u32[]{:S(2)}, u32[]{:S(2)}) collective-permute-start(f32[1,4,1,2048]{3,2,1,0:T(1,128)} %get-tuple-element.20), channel_id=1, source_target_pairs={{1,0},{2,1},{3,2},{4,3},{5,4},{6,5},{7,6},{9,8},{10,9},{11,10},{12... | collective-permute-start | bytes 98312 | tf_op jit(solution)/shard_map/ppermute | solution.py:18
  16.3 14.7 %copy-start = (s32[64,2]{0,1:T(2,128)S(1)}, s32[64,2]{0,1:T(2,128)}, u32[]{:S(2)}) copy-start(s32[64,2]{0,1:T(2,128)} %param.11) | copy-start | bytes 1540
  16.3 15.0 %copy-start.1 = (f32[64,2]{0,1:T(2,128)S(1)}, f32[64,2]{0,1:T(2,128)}, u32[]{:S(2)}) copy-start(f32[64,2]{0,1:T(2,128)} %param.13) | copy-start | bytes 1540
  16.3 15.2 %copy-start.2 = (s32[64,2]{0,1:T(2,128)S(1)}, s32[64,2]{0,1:T(2,128)}, u32[]{:S(2)}) copy-start(s32[64,2]{0,1:T(2,128)} %param.12) | copy-start | bytes 1540
  29.6 45.2 %copy-start.3 = (f32[4]{0:T(128)S(1)}, f32[4]{0:T(128)}, u32[]{:S(2)}) copy-start(f32[4]{0:T(128)} %param.10) | copy-start | bytes 52
  37.8 5.6 %collective-permute-start.3 = (f32[64,128]{0,1:T(8,128)S(1)}, f32[64,128]{0,1:T(8,128)S(1)}, u32[]{:S(2)}, u32[]{:S(2)}) collective-permute-start(f32[64,128]{0,1:T(8,128)S(1)} %collective-permute-done.2), channel_id=1, source_target_pairs={{0,1},{1,2},{2,3},{3,4},{4,5},{5,6},{6,7},{7,0},{8,9},{9,10},{10,1... | collective-permute-start | bytes 98312 | tf_op jit(solution)/shard_map/ppermute | solution.py:79
  39.0 5.1 %collective-permute-start.7 = (f32[64,128]{0,1:T(8,128)S(1)}, f32[64,128]{0,1:T(8,128)S(1)}, u32[]{:S(2)}, u32[]{:S(2)}) collective-permute-start(f32[64,128]{0,1:T(8,128)S(1)} %collective-permute-done.6), channel_id=1, source_target_pairs={{0,7},{1,0},{2,1},{3,2},{4,3},{5,4},{6,5},{7,6},{8,15},{9,8},{10,9... | collective-permute-start | bytes 98312 | tf_op jit(solution)/shard_map/ppermute | solution.py:81
  43.4 5.6 %collective-permute-start.4 = (f32[64,128]{0,1:T(8,128)S(1)}, f32[64,128]{0,1:T(8,128)S(1)}, u32[]{:S(2)}, u32[]{:S(2)}) collective-permute-start(f32[64,128]{0,1:T(8,128)S(1)} %collective-permute-done.3), channel_id=1, source_target_pairs={{0,1},{1,2},{2,3},{3,4},{4,5},{5,6},{6,7},{7,0},{8,9},{9,10},{10,1... | collective-permute-start | bytes 98312 | tf_op jit(solution)/shard_map/ppermute | solution.py:79
  44.0 25.4 %collective-permute-start.8 = (f32[64,128]{0,1:T(8,128)S(1)}, f32[64,128]{0,1:T(8,128)}, u32[]{:S(2)}, u32[]{:S(2)}) collective-permute-start(f32[64,128]{0,1:T(8,128)S(1)} %collective-permute-done.7), channel_id=1, source_target_pairs={{0,7},{1,0},{2,1},{3,2},{4,3},{5,4},{6,5},{7,6},{8,15},{9,8},{10,9... | collective-permute-start | bytes 98312 | tf_op jit(solution)/shard_map/ppermute | solution.py:81
  49.0 20.5 %collective-permute-start.5 = (f32[64,128]{0,1:T(8,128)S(1)}, f32[64,128]{0,1:T(8,128)}, u32[]{:S(2)}, u32[]{:S(2)}) collective-permute-start(f32[64,128]{0,1:T(8,128)S(1)} %collective-permute-done.4), channel_id=1, source_target_pairs={{0,1},{1,2},{2,3},{3,4},{4,5},{5,6},{6,7},{7,0},{8,9},{9,10},{10,1... | collective-permute-start | bytes 98312 | tf_op jit(solution)/shard_map/ppermute | solution.py:79
Sparse Core Ops, SparseCore 0:
  74.9 26.6 reduce-scatter.1
